TPU v7x, 32 devices: a whole 2x2x4 slice. The times are simulated.
32 devices in a mesh: srv: 8 (over y, x, core), head: 4 (over z).
Axes of the slice: x: 2, y: 2, z: 4, core: 2. Of those that a mesh axis runs over, the one named last changes fastest.
Arguments:
- queries: bfloat16 [2048, 8192], P('srv', 'head'), may hold values from -200 to 200
- key_value_pair: bfloat16 [2, 2048, 1024], P(None, 'srv', 'head'), may hold values from -200 to 200
- lengths: int32 [8], replicated, may hold values from 1 to 1024, 2048 in all
Outputs:
- attended: bfloat16 [2048, 8192], P(('srv', 'head'))
All inputs are finite; a program needn't handle non-finite values.
Results may differ from a plain program's by a relative error of at most 0.012.
Values may be sent and summed in bfloat16 or wider, within the bound.
A program may use at most 64 MiB of HBM per device.

v0:
```python
import functools
import math

import jax
import jax.numpy as jnp
from jax import lax
from jax.experimental import pallas as pl
from jax.experimental.pallas import tpu as pltpu
from jax.sharding import PartitionSpec as P

HEAD = 128
MESH = pl.DeviceIdType.MESH


def kernel(cfg, len_ref, q_ref, kv_ref, out_ref, qraw, qrot, kvbuf, kvin, ksend, table, bias, obuf,
           lsem, qs, qr, kvs, kvr, fwd, osend, orecv):
    n_srv, n_head, G, back, tok, kvh, per, R, chunk, ndoc = cfg
    heads = kvh * per
    grp = G * tok
    n_grp = n_srv // G
    T = tok // n_head
    longest = back * grp
    W = longest + R
    width = heads * HEAD
    kw = kvh * HEAD
    nblk = grp // R
    nch = heads // chunk
    per_blk = R // T
    cw = chunk * HEAD
    srv = lax.axis_index("srv")
    z = lax.axis_index("head")
    k = srv // G
    a = srv % G

    bar = pltpu.get_barrier_semaphore()

    def greet(s, h):
        pl.semaphore_signal(bar, inc=1, device_id=(s, h), device_id_type=MESH)

    for i in range(1, n_head):
        for b in range(G):
            greet(k * G + b, (z + i) % n_head)
    for i in range(1, G):
        greet(k * G + (a + i) % G, z)
    for d in range(1, back + 1):
        @pl.when(k + d < n_grp)
        def _():
            for b in range(G):
                greet((k + d) * G + b, z)

        @pl.when(k - d >= 0)
        def _():
            for b in range(G):
                greet((k - d) * G + b, z)

    own_kv = pltpu.make_async_copy(kv_ref, kvin, lsem.at[0])
    own_kv.start()
    my_cols = pl.ds(pl.multiple_of(a * width, HEAD), width)
    own_q = pltpu.make_async_copy(q_ref.at[:, my_cols], qraw.at[a], lsem.at[1])
    own_q.start()

    for d in range(1, back + 1):
        @pl.when(k - d < 0)
        def _():
            kvbuf[:, pl.ds((back - d) * grp, grp), :] = jnp.zeros((2, grp, kw), jnp.bfloat16)

    ends = []
    total = jnp.int32(0)
    for i in range(ndoc):
        total = total + len_ref[i]
        ends.append(total)

    lane = lax.broadcasted_iota(jnp.int32, (tok, HEAD), 1)
    low = lane < HEAD // 2
    step_up = jnp.where(low, lane, lane - HEAD // 2).astype(jnp.float32) * (2.0 / HEAD)
    inverse = jnp.exp(-step_up * math.log(500000.0))

    def starts_of(rows):
        start = jnp.zeros_like(rows)
        for e in ends:
            start = jnp.where(e <= rows, e, start)
        return start

    def make_table(b):
        rows = (k * G + b) * tok + lax.broadcasted_iota(jnp.int32, (tok, HEAD), 0)
        angle = (rows - starts_of(rows)).astype(jnp.float32) * inverse
        sine = jnp.sin(angle)
        table[0] = jnp.cos(angle)
        table[1] = jnp.where(low, -sine, sine)

    def rotate(x):
        x = x.astype(jnp.float32)
        return (x * table[0] + pltpu.roll(x, HEAD // 2, 1) * table[1]).astype(jnp.bfloat16)

    make_table(a)
    own_kv.wait()
    for h in range(G * kvh):
        cols = slice(h * HEAD, (h + 1) * HEAD)
        ksend[:, cols] = rotate(kvin[0, :, cols])

    own_rows = pl.ds(pl.multiple_of(back * grp + a * tok, tok), tok)
    kv_cols = pl.ds(pl.multiple_of(a * kw, HEAD), kw)
    kvbuf[0, own_rows, :] = ksend[:, kv_cols]
    kvbuf[1, own_rows, :] = kvin[1, :, kv_cols]

    count = (n_head - 1) * G + (G - 1)
    for d in range(1, back + 1):
        count = count + G * jnp.where(k + d < n_grp, 1, 0) + G * jnp.where(k - d >= 0, 1, 0)
    pl.semaphore_wait(bar, count)

    def kv_copy(d, i, which):
        b = (a + i) % G
        cols = pl.ds(pl.multiple_of(b * kw, HEAD), kw)
        src = ksend.at[:, cols] if which == 0 else kvin.at[1, :, cols]
        rows = pl.ds(pl.multiple_of((back - d) * grp + a * tok, tok), tok)
        return pltpu.make_async_remote_copy(
            src_ref=src, dst_ref=kvbuf.at[which, rows, :],
            send_sem=kvs.at[d, i, which], recv_sem=kvr.at[d, a, which],
            device_id=((k + d) * G + b, z), device_id_type=MESH)

    def kv_wait(d, b, which):
        rows = pl.ds(pl.multiple_of((back - d) * grp + b * tok, tok), tok)
        ref = kvbuf.at[which, rows, :]
        pltpu.make_async_copy(ref, ref, kvr.at[d, b, which]).wait()

    relayed = jnp.logical_and(jnp.logical_and(k % 2 == 1, k + 2 < n_grp), a == G - 1)
    relays = jnp.logical_and(k % 2 == 1, k >= 3)

    def sends(d):
        near = k + d < n_grp
        if d == 1 and back >= 2:
            near = jnp.logical_and(near, jnp.logical_not(relayed))
        return near

    def relay_copy(b, which):
        src = pl.ds(pl.multiple_of((back - 2) * grp + b * tok, tok), tok)
        dst = pl.ds(pl.multiple_of((back - 1) * grp + b * tok, tok), tok)
        return pltpu.make_async_remote_copy(
            src_ref=kvbuf.at[which, src, :], dst_ref=kvbuf.at[which, dst, :],
            send_sem=fwd.at[b, which], recv_sem=kvr.at[1, b, which],
            device_id=(srv - G, z), device_id_type=MESH)

    def start_kv(d, when):
        @pl.when(jnp.logical_and(sends(d), when))
        def _():
            pairs = [(i, which) for which in range(2) for i in range(G)]
            for i, which in pairs if d == 1 else sorted(pairs):
                kv_copy(d, i, which).start()

    for d in range(1, back + 1):
        start_kv(d, a == G - 1 if d == back else True)
    q_copies = []
    for i in range(1, G):
        b = (a + i) % G
        for which in range(2):
            kv_copy(0, i, which).start()
        cols = pl.ds(pl.multiple_of(b * width, HEAD), width)
        c = pltpu.make_async_remote_copy(
            src_ref=q_ref.at[:, cols], dst_ref=qraw.at[a],
            send_sem=qs.at[i], recv_sem=qr.at[a],
            device_id=(k * G + b, z), device_id_type=MESH)
        c.start()
        q_copies.append(c)

    def rotate_queries(b):
        for h in range(heads):
            qrot[h, pl.ds(pl.multiple_of(b * tok, tok), tok), :] = rotate(
                qraw[b, :, h * HEAD:(h + 1) * HEAD])

    own_q.wait()
    rotate_queries(a)
    start_kv(back, a < G - 1)
    for i in range(1, G):
        b = (a + i) % G
        make_table(b)
        pltpu.make_async_copy(qraw.at[b], qraw.at[b], qr.at[b]).wait()
        rotate_queries(b)

    if back >= 2:
        @pl.when(k >= 2)
        def _():
            kv_wait(2, G - 1, 0)

            @pl.when(relays)
            def _():
                relay_copy(G - 1, 0).start()
                kv_wait(2, G - 1, 1)
                relay_copy(G - 1, 1).start()

    def wait_early(which):
        for i in range(1, G):
            kv_wait(0, (a + i) % G, which)
        if which == 1 and back >= 2:
            @pl.when(jnp.logical_and(k >= 2, jnp.logical_not(relays)))
            def _():
                kv_wait(2, G - 1, 1)
        for d in range(1, back + 1):
            @pl.when(k - d >= 0)
            def _():
                for b in range(G - 1 if d == back else 0, G):
                    if (d, b) != (2, G - 1):
                        kv_wait(d, b, which)

    def wait_late():
        @pl.when(k - back >= 0)
        def _():
            for b in range(G - 1):
                for which in range(2):
                    kv_wait(back, b, which)

    wait_early(0)

    nbm = tok // R
    zpart = z * nbm // n_head
    edge = n_head // 4
    outer = jnp.logical_or(z < edge, z >= n_head - edge)
    scale = HEAD ** -0.5 * math.log2(math.e)

    def where_of(s):
        blk = s // nch
        c = s % nch
        late = jnp.where(blk == 0, 0, jnp.where(blk == nblk - 1, 1, blk + 1))
        blk = jnp.where(outer, late, blk)
        b = G - 1 - blk % G
        part = (zpart + 1 + blk // G) % nbm
        return blk, c, b, part

    def out_copy(s, j):
        blk, c, b, part = where_of(s)
        dest = part * per_blk + j
        col = pl.multiple_of(z * (G * width) + a * width + c * cw, HEAD)
        src = obuf.at[s, pl.ds(j * T, T), :]
        dst = out_ref.at[:, pl.ds(col, cw)]
        idx = (z * G + a) * nch + c
        remote = pltpu.make_async_remote_copy(
            src_ref=src, dst_ref=dst, send_sem=osend.at[s * per_blk + j], recv_sem=orecv.at[idx],
            device_id=(k * G + b, dest), device_id_type=MESH)
        local = pltpu.make_async_copy(src, dst, orecv.at[idx])
        mine = jnp.logical_and(b == a, dest == z)
        return mine, remote, local

    def one_step(s, carry):
        blk, c, b, part = where_of(s)
        r0 = pl.multiple_of(b * tok + part * R, R)

        @pl.when(s == nch)
        def _():
            wait_late()

        @pl.when(c == 0)
        def _():
            rows = k * grp + r0 + lax.broadcasted_iota(jnp.int32, (R, HEAD), 0)
            start = starts_of(rows)
            for j in range(W // HEAD):
                t = (k - back) * grp + r0 + j * HEAD + lax.broadcasted_iota(jnp.int32, (R, HEAD), 1)
                ok = jnp.logical_and(t >= start, t <= rows)
                bias[:, j * HEAD:(j + 1) * HEAD] = jnp.where(ok, 0.0, -1e30)

        kcol = pl.ds(pl.multiple_of((c * chunk // per) * HEAD, HEAD), HEAD)
        keys = kvbuf[0, pl.ds(r0, W), kcol]
        q = qrot[pl.ds(c * chunk, chunk), pl.ds(r0, R), :].reshape(chunk * R, HEAD)
        sc = lax.dot_general(q, keys, (((1,), (1,)), ((), ())), preferred_element_type=jnp.float32)
        sc = (sc.reshape(chunk, R, W) + bias[...][None]).reshape(chunk * R, W)
        top = jnp.max(sc, axis=1, keepdims=True)
        w = jnp.exp2((sc - top) * scale).astype(jnp.bfloat16)

        @pl.when(s == 0)
        def _():
            wait_early(1)

        vals = kvbuf[1, pl.ds(r0, W), kcol]
        vals = jnp.concatenate([vals, jnp.ones_like(vals)], axis=1)
        acc = lax.dot_general(w, vals, (((1,), (0,)), ((), ())), preferred_element_type=jnp.float32)
        o = (acc[:, :HEAD] / acc[:, HEAD:]).astype(jnp.bfloat16)
        for h in range(chunk):
            obuf[s, :, h * HEAD:(h + 1) * HEAD] = o[h * R:(h + 1) * R, :]

        for j in range(per_blk):
            mine, remote, local = out_copy(s, j)

            @pl.when(mine)
            def _():
                local.start()

            @pl.when(jnp.logical_not(mine))
            def _():
                remote.start()
        return carry

    lax.fori_loop(0, nblk * nch, one_step, 0)

    for i in range(1, G):
        for which in (1, 0):
            kv_copy(0, i, which).wait_send()
    for c in q_copies:
        c.wait_send()
    for d in range(1, back + 1):
        @pl.when(sends(d))
        def _():
            for i in range(G):
                for which in (1, 0):
                    kv_copy(d, i, which).wait_send()
    if back >= 2:
        @pl.when(relays)
        def _():
            for which in range(2):
                relay_copy(G - 1, which).wait_send()

    def end_send(s, carry):
        for j in range(per_blk):
            mine, remote, local = out_copy(s, j)

            @pl.when(jnp.logical_not(mine))
            def _():
                remote.wait_send()
        return carry

    lax.fori_loop(0, nblk * nch, end_send, 0)

    def end_recv(i, carry):
        col = pl.multiple_of(i * cw, HEAD)
        ref = out_ref.at[:, pl.ds(col, cw)]
        pltpu.make_async_copy(ref, ref, orecv.at[i]).wait()
        return carry

    lax.fori_loop(0, n_head * G * nch, end_recv, 0)


def solution(mesh):
    n_srv, n_head = mesh.shape["srv"], mesh.shape["head"]

    def body(queries, key_value_pair, lengths):
        tok, qw = queries.shape
        kv_all = key_value_pair.shape[2] // HEAD
        G = 2 if kv_all % 2 == 0 and n_srv % 2 == 0 else 1
        kvh = kv_all // G
        per = qw // HEAD // kv_all
        grp = G * tok
        n_grp = n_srv // G
        back = n_grp // 2
        T = tok // n_head
        R = max(tok // 2, T)
        chunk = per // 2
        ndoc = lengths.shape[0]
        heads = kvh * per
        nsteps = (grp // R) * (heads // chunk)
        W = back * grp + R
        cfg = (n_srv, n_head, G, back, tok, kvh, per, R, chunk, ndoc)
        bf = jnp.bfloat16
        dma = pltpu.SemaphoreType.DMA
        return pl.pallas_call(
            functools.partial(kernel, cfg),
            out_shape=pltpu.VMEM((T, qw * n_head), bf),
            in_specs=[
                pl.BlockSpec(memory_space=pltpu.SMEM),
                pl.BlockSpec(memory_space=pl.ANY),
                pl.BlockSpec(memory_space=pl.ANY),
            ],
            out_specs=pl.BlockSpec(memory_space=pl.ANY),
            scratch_shapes=[
                pltpu.VMEM((G, tok, heads * HEAD), bf),
                pltpu.VMEM((heads, grp, HEAD), bf),
                pltpu.VMEM((2, (back + 1) * grp, kvh * HEAD), bf),
                pltpu.VMEM((2, tok, kv_all * HEAD), bf),
                pltpu.VMEM((tok, kv_all * HEAD), bf),
                pltpu.VMEM((2, tok, HEAD), jnp.float32),
                pltpu.VMEM((R, W), jnp.float32),
                pltpu.VMEM((nsteps, R, chunk * HEAD), bf),
                dma((2,)),
                dma((G,)),
                dma((G,)),
                dma((back + 1, G, 2)),
                dma((back + 1, G, 2)),
                dma((G, 2)),
                dma((nsteps * (R // T),)),
                dma((n_head * G * (heads // chunk),)),
            ],
            compiler_params=pltpu.CompilerParams(collective_id=0, has_side_effects=True),
            name="attend",
        )(lengths, queries, key_value_pair)

    in_specs = (P("srv", "head"), P(None, "srv", "head"), P())
    out_specs = P(("srv", "head"), None)
    return jax.shard_map(body, mesh=mesh, in_specs=in_specs, out_specs=out_specs, check_vma=False)
```

profile of v0, /device:TPU:10, one launch (start us, length us, event | category | flops | bytes accessed | tf_op | source)
XLA Modules:
  0.0 36.5 jit_solution(2472418934156758766)
XLA Ops:
  0.0 35.6 %attend.1 = bf16[64,8192]{1,0:T(8,128)(2,1)S(1)} custom-call(s32[8]{0:T(128)} %len_ref.1, bf16[256,2048]{1,0:T(8,128)(2,1)} %q_ref.1, bf16[2,256,256]{2,1,0:T(8,128)(2,1)} %kv_ref.1), custom_call_target="tpu_custom_call" | custom-call | tf_op jit(solution)/shard_map/attend/pallas_call | solution.py:351
  35.6 1.0 %copy.5 = bf16[64,8192]{1,0:T(8,128)(2,1)} copy(bf16[64,8192]{1,0:T(8,128)(2,1)S(1)} %attend.1) | data formatting | bytes 2097152
where the time goes:
time: 37 us; the launch traced here: 36.5 us
  Pallas kernels  35.6 us (96%)
  local copies, waits for them, and re-layouts  0.97 us (3%)
    pallas_call x1, Pallas kernels, body(): pl.pallas_call(functools.partial(kernel, cfg), out_shape=pltpu.VMEM((T, q...  35.6 us
    unnamed x1, local copies, waits for them, and re-layouts  0.97 us

commit v1 on v0

v1 whole, which is shorter than its diff:
```python
import functools
import math

import jax
import jax.numpy as jnp
from jax import lax
from jax.experimental import pallas as pl
from jax.experimental.pallas import tpu as pltpu
from jax.sharding import PartitionSpec as P

HEAD = 128
MESH = pl.DeviceIdType.MESH


def kernel(cfg, len_ref, q_ref, kv_ref, out_ref, qraw, qrot, kvbuf, kvin, ksend, fkv, table, bias,
           sc0, mx0, obuf, lsem, qs, qr, kvs, kvr, fwd, xs, xr, fs, fr, hs, osend, orecv):
    n_srv, n_head, G, back, tok, kvh, per, R, chunk, ndoc, swap = cfg
    heads = kvh * per
    grp = G * tok
    n_grp = n_srv // G
    T = tok // n_head
    longest = back * grp
    W = longest + R
    width = heads * HEAD
    kw = kvh * HEAD
    nbm = tok // R
    nblk = grp // R
    nch = heads // chunk
    units = nblk * nch
    per_blk = R // T
    cw = chunk * HEAD
    rows_u = chunk * R
    srv = lax.axis_index("srv")
    z = lax.axis_index("head")
    k = srv // G
    a = srv % G

    mine_half = z // (n_head // nbm)
    partner = n_head - 1 - z
    if swap:
        inner = jnp.logical_or(z == n_head // 2 - 1, z == n_head // 2)
    else:
        inner = z < 0
    swapped = jnp.logical_and(inner, a == G - 1)

    bar = pltpu.get_barrier_semaphore()

    def greet(s, h):
        pl.semaphore_signal(bar, inc=1, device_id=(s, h), device_id_type=MESH)

    for i in range(1, n_head):
        for b in range(G):
            greet(k * G + b, (z + i) % n_head)
    for i in range(1, G):
        greet(k * G + (a + i) % G, z)
    for d in range(1, back + 1):
        @pl.when(k + d < n_grp)
        def _():
            for b in range(G):
                greet((k + d) * G + b, z)

        @pl.when(k - d >= 0)
        def _():
            for b in range(G):
                greet((k - d) * G + b, z)

    own_kv = pltpu.make_async_copy(kv_ref, kvin, lsem.at[0])
    own_kv.start()

    def cols_of(b):
        return pl.ds(pl.multiple_of(b * width, HEAD), width)

    def part_rows(p):
        return slice(p * R, (p + 1) * R)

    def own_q(p):
        return pltpu.make_async_copy(q_ref.at[part_rows(p), cols_of(a)], qraw.at[a, p], qr.at[a, p])

    def kept(p):
        return jnp.logical_not(jnp.logical_and(swapped, mine_half != p))

    for p in range(nbm):
        @pl.when(kept(p))
        def _():
            own_q(p).start()

    ends = []
    total = jnp.int32(0)
    for i in range(ndoc):
        total = total + len_ref[i]
        ends.append(total)

    lane = lax.broadcasted_iota(jnp.int32, (tok, HEAD), 1)
    low = lane < HEAD // 2
    step_up = jnp.where(low, lane, lane - HEAD // 2).astype(jnp.float32) * (2.0 / HEAD)
    inverse = jnp.exp(-step_up * math.log(500000.0))

    def starts_of(rows):
        start = jnp.zeros_like(rows)
        for e in ends:
            start = jnp.where(e <= rows, e, start)
        return start

    def cos_sin(angle):
        turns = jnp.floor(angle * (2.0 / math.pi) + 0.5)
        r = ((angle - turns * 1.5703125) - turns * 4.837512969970703125e-4) - turns * 7.549789948768648e-8
        r2 = r * r
        s = r + r * r2 * (-1.6666654611e-1 + r2 * (8.3321608736e-3 - r2 * 1.9515295891e-4))
        c = 1.0 - 0.5 * r2 + r2 * r2 * (
            4.166664568298827e-2 + r2 * (-1.388731625493765e-3 + r2 * 2.443315711809948e-5))
        quarter = turns.astype(jnp.int32)
        odd = (quarter & 1) == 1
        sine = jnp.where(odd, c, s)
        cosine = jnp.where(odd, s, c)
        sine = jnp.where((quarter & 2) == 2, -sine, sine)
        cosine = jnp.where(((quarter + 1) & 2) == 2, -cosine, cosine)
        return cosine, sine

    def make_table(b):
        rows = (k * G + b) * tok + lax.broadcasted_iota(jnp.int32, (tok, HEAD), 0)
        angle = (rows - starts_of(rows)).astype(jnp.float32) * inverse
        cosine, sine = cos_sin(angle)
        table[b, 0] = cosine
        table[b, 1] = jnp.where(low, -sine, sine)

    def rotate(x, cosine, sine):
        x = x.astype(jnp.float32)
        return (x * cosine + pltpu.roll(x, HEAD // 2, 1) * sine).astype(jnp.bfloat16)

    make_table(a)
    own_kv.wait()
    for h in range(G * kvh):
        cols = slice(h * HEAD, (h + 1) * HEAD)
        ksend[:, cols] = rotate(kvin[0, :, cols], table[a, 0], table[a, 1])

    own_rows = pl.ds(pl.multiple_of(back * grp + a * tok, tok), tok)
    kv_cols = pl.ds(pl.multiple_of(a * kw, HEAD), kw)
    kvbuf[0, 0, own_rows, :] = ksend[:, kv_cols]
    kvbuf[0, 1, own_rows, :] = kvin[1, :, kv_cols]

    count = (n_head - 1) * G + (G - 1)
    for d in range(1, back + 1):
        count = count + G * jnp.where(k + d < n_grp, 1, 0) + G * jnp.where(k - d >= 0, 1, 0)
    pl.semaphore_wait(bar, count)

    def kv_copy(d, i, which):
        b = (a + i) % G
        cols = pl.ds(pl.multiple_of(b * kw, HEAD), kw)
        src = ksend.at[:, cols] if which == 0 else kvin.at[1, :, cols]
        rows = pl.ds(pl.multiple_of((back - d) * grp + a * tok, tok), tok)
        return pltpu.make_async_remote_copy(
            src_ref=src, dst_ref=kvbuf.at[0, which, rows, :],
            send_sem=kvs.at[d, i, which], recv_sem=kvr.at[d, a, which],
            device_id=((k + d) * G + b, z), device_id_type=MESH)

    def kv_wait(d, b, which):
        rows = pl.ds(pl.multiple_of((back - d) * grp + b * tok, tok), tok)
        ref = kvbuf.at[0, which, rows, :]
        pltpu.make_async_copy(ref, ref, kvr.at[d, b, which]).wait()

    odd_near = jnp.logical_and(k % 2 == 1, k + 2 < n_grp)
    relayed = jnp.logical_and(odd_near, a == G - 1)
    relays = jnp.logical_and(k % 2 == 1, k >= 3)

    def sends(d):
        near = k + d < n_grp
        if d == 1 and back >= 2:
            near = jnp.logical_and(near, jnp.logical_not(relayed))
        return near

    def relay_copy(b, which):
        src = pl.ds(pl.multiple_of((back - 2) * grp + b * tok, tok), tok)
        dst = pl.ds(pl.multiple_of((back - 1) * grp + b * tok, tok), tok)
        return pltpu.make_async_remote_copy(
            src_ref=kvbuf.at[0, which, src, :], dst_ref=kvbuf.at[0, which, dst, :],
            send_sem=fwd.at[b, which], recv_sem=kvr.at[1, b, which],
            device_id=(srv - G, z), device_id_type=MESH)

    def start_kv(d, when):
        @pl.when(jnp.logical_and(sends(d), when))
        def _():
            pairs = [(i, which) for which in range(2) for i in range(G)]
            for i, which in pairs if d == 1 else sorted(pairs):
                kv_copy(d, i, which).start()

    moved = pl.ds((G - 1) * kw, kw)

    def cross_kv(which):
        src = ksend.at[:, moved] if which == 0 else kvin.at[1, :, moved]
        return pltpu.make_async_remote_copy(
            src_ref=src, dst_ref=fkv.at[which], send_sem=xs.at[which], recv_sem=xr.at[which],
            device_id=(srv, partner), device_id_type=MESH)

    def cross_q():
        there = nbm - 1 - mine_half
        src = pl.ds(pl.multiple_of(there * R, R), R)
        return pltpu.make_async_remote_copy(
            src_ref=q_ref.at[src, pl.ds((G - 1) * width, width)], dst_ref=qraw.at[a, mine_half],
            send_sem=xs.at[2], recv_sem=qr.at[a, mine_half],
            device_id=(k * G + G - 1, partner), device_id_type=MESH)

    def chip_q(i, p):
        b = (a + i) % G
        return pltpu.make_async_remote_copy(
            src_ref=q_ref.at[part_rows(p), cols_of(b)], dst_ref=qraw.at[a, p],
            send_sem=qs.at[i, p], recv_sem=qr.at[a, p],
            device_id=(k * G + b, z), device_id_type=MESH)

    def chip_kept(i, p):
        b = (a + i) % G
        away = jnp.logical_and(jnp.logical_and(inner, b == G - 1), mine_half != p)
        return jnp.logical_not(away)

    for d in range(1, back + 1):
        start_kv(d, a == G - 1 if d == back else True)
    if swap:
        @pl.when(inner)
        def _():
            cross_kv(0).start()
            cross_kv(1).start()
            cross_q().start()
    for i in range(1, G):
        for which in range(2):
            kv_copy(0, i, which).start()
        for p in range(nbm):
            @pl.when(chip_kept(i, p))
            def _():
                chip_q(i, p).start()

    def q_wait(b, p):
        pltpu.make_async_copy(qraw.at[b, p], qraw.at[b, p], qr.at[b, p]).wait()

    def rotate_queries(b, p, part):
        rows = pl.ds(pl.multiple_of(part * R, R), R)
        cosine = table[b, 0, rows, :]
        sine = table[b, 1, rows, :]
        dst = pl.ds(pl.multiple_of((b * nbm + p) * R, R), R)
        for h in range(heads):
            qrot[h, dst, :] = rotate(qraw[b, p, :, h * HEAD:(h + 1) * HEAD], cosine, sine)

    def take_queries(b):
        for p in range(nbm):
            @pl.when(kept(p))
            def _():
                q_wait(b, p)
                rotate_queries(b, p, p)

    for d in range(1, back + 1):
        @pl.when(k - d < 0)
        def _():
            for sel in range(2 if swap else 1):
                kvbuf[sel, :, pl.ds((back - d) * grp, grp), :] = jnp.zeros((2, grp, kw), jnp.bfloat16)

    take_queries(a)
    start_kv(back, a < G - 1)
    for i in range(1, G):
        b = (a + i) % G
        make_table(b)
        take_queries(b)

    def pass_copy(d, which):
        rows = pl.ds(pl.multiple_of((back - d) * grp + a * tok, tok), tok)
        return pltpu.make_async_remote_copy(
            src_ref=fkv.at[which], dst_ref=kvbuf.at[1, which, rows, :],
            send_sem=fs.at[d, which], recv_sem=fr.at[d, a, which],
            device_id=((k + d) * G + G - 1, z), device_id_type=MESH)

    def passes(d):
        if d == 0:
            return a < G - 1
        near = k + d < n_grp
        if d == 1 and back >= 2:
            near = jnp.logical_and(near, jnp.logical_not(odd_near))
        return near

    hands_on = jnp.logical_and(relays, swapped)

    def hand_copy(b, which):
        src = pl.ds(pl.multiple_of((back - 2) * grp + b * tok, tok), tok)
        dst = pl.ds(pl.multiple_of((back - 1) * grp + b * tok, tok), tok)
        return pltpu.make_async_remote_copy(
            src_ref=kvbuf.at[1, which, src, :], dst_ref=kvbuf.at[1, which, dst, :],
            send_sem=hs.at[b, which], recv_sem=fr.at[1, b, which],
            device_id=(srv - G, z), device_id_type=MESH)

    def moved_wait(d, b, which):
        rows = pl.ds((back - d) * grp + b * tok, tok)
        ref = kvbuf.at[1, which, rows, :]
        pltpu.make_async_copy(ref, ref, fr.at[d, b, which]).wait()

    def pass_on(which):
        @pl.when(inner)
        def _():
            pltpu.make_async_copy(fkv.at[which], fkv.at[which], xr.at[which]).wait()
            for d in range(back, -1, -1):
                @pl.when(passes(d))
                def _():
                    pass_copy(d, which).start()

            @pl.when(swapped)
            def _():
                kvbuf[1, which, own_rows, :] = fkv[which]

    for which in range(2):
        if back >= 2:
            @pl.when(relays)
            def _():
                kv_wait(2, G - 1, which)
                relay_copy(G - 1, which).start()
        if swap:
            pass_on(which)

    def wait_moved():
        for which in range(2):
            for d in range(back + 1):
                for b in range(G):
                    if d == 0:
                        if b < G - 1:
                            moved_wait(d, b, which)
                    else:
                        ready = k - d >= 0
                        if d == 2:
                            ready = jnp.logical_and(ready, jnp.logical_not(relays))

                        @pl.when(ready)
                        def _():
                            moved_wait(d, b, which)

    def kv_wait_new(d, b, which):
        if (d, b) == (2, G - 1):
            @pl.when(jnp.logical_not(relays))
            def _():
                kv_wait(d, b, which)
        else:
            kv_wait(d, b, which)

    def wait_early(which):
        for i in range(1, G):
            kv_wait(0, (a + i) % G, which)
        for d in range(1, back + 1):
            @pl.when(k - d >= 0)
            def _():
                for b in range(G - 1 if d == back else 0, G):
                    kv_wait_new(d, b, which)

    def wait_late():
        @pl.when(k - back >= 0)
        def _():
            for b in range(G - 1):
                for which in range(2):
                    kv_wait_new(back, b, which)

    wait_early(0)

    edge = n_head // 4
    outer = jnp.logical_or(z < edge, z >= n_head - edge)
    scale = HEAD ** -0.5 * math.log2(math.e)

    def where_of(u):
        blk = u // nch
        c = u % nch
        late = jnp.where(blk == 0, 0, jnp.where(blk == nblk - 1, 1, blk + 1))
        blk = jnp.where(outer, late, blk)
        b = G - 1 - blk % G
        slot = (mine_half + jnp.where(swapped, 0, 1) + blk // G) % nbm
        foreign = jnp.where(jnp.logical_and(swapped, slot != mine_half), 1, 0)
        part = jnp.where(foreign == 1, mine_half, slot)
        return c, b, slot, part, foreign

    def make_bias(u):
        c, b, slot, part, foreign = where_of(u)
        r0 = pl.multiple_of(b * tok + part * R, R)
        rows = k * grp + r0 + lax.broadcasted_iota(jnp.int32, (R, HEAD), 0)
        start = starts_of(rows)
        for j in range(W // HEAD):
            t = (k - back) * grp + r0 + j * HEAD + lax.broadcasted_iota(jnp.int32, (R, HEAD), 1)
            ok = jnp.logical_and(t >= start, t <= rows)
            bias[:, j * HEAD:(j + 1) * HEAD] = jnp.where(ok, 0.0, -1e30)

    def scores(u, sc, mx):
        c, b, slot, part, foreign = where_of(u)
        r0 = pl.multiple_of(b * tok + part * R, R)
        q0 = pl.multiple_of((b * nbm + slot) * R, R)
        kcol = pl.ds(pl.multiple_of((c * chunk // per) * HEAD, HEAD), HEAD)
        q = qrot[pl.ds(c * chunk, chunk), pl.ds(q0, R), :].reshape(rows_u, HEAD)
        top = None
        for t0 in range(0, W, 2 * HEAD):
            n = min(2 * HEAD, W - t0)
            keys = kvbuf[foreign, 0, pl.ds(pl.multiple_of(r0 + t0, HEAD), n), kcol]
            s = lax.dot_general(q, keys, (((1,), (1,)), ((), ())), preferred_element_type=jnp.float32)
            s = (s.reshape(chunk, R, n) + bias[:, t0:t0 + n][None]).reshape(rows_u, n)
            sc[:, t0:t0 + n] = s
            m = functools.reduce(jnp.maximum, [s[:, h:h + HEAD] for h in range(0, n, HEAD)])
            top = m if top is None else jnp.maximum(top, m)
        mx[...] = jnp.broadcast_to(jnp.max(top, axis=1, keepdims=True), (rows_u, HEAD))

    def attend(u, sc, mx):
        c, b, slot, part, foreign = where_of(u)
        r0 = pl.multiple_of(b * tok + part * R, R)
        kcol = pl.ds(pl.multiple_of((c * chunk // per) * HEAD, HEAD), HEAD)
        top = mx[...]
        acc = None
        for t0 in range(0, W, 2 * HEAD):
            n = min(2 * HEAD, W - t0)
            peak = jnp.concatenate([top] * (n // HEAD), axis=1)
            w = jnp.exp2((sc[:, t0:t0 + n] - peak) * scale).astype(jnp.bfloat16)
            vals = kvbuf[foreign, 1, pl.ds(pl.multiple_of(r0 + t0, HEAD), n), kcol]
            vals = jnp.concatenate([vals, jnp.ones_like(vals)], axis=1)
            part_acc = lax.dot_general(w, vals, (((1,), (0,)), ((), ())), preferred_element_type=jnp.float32)
            acc = part_acc if acc is None else acc + part_acc
        o = (acc[:, :HEAD] / acc[:, HEAD:]).astype(jnp.bfloat16)
        for h in range(chunk):
            obuf[u, :, h * HEAD:(h + 1) * HEAD] = o[h * R:(h + 1) * R, :]

    def out_copy(u, j):
        c, b, slot, part, foreign = where_of(u)
        dest = part * per_blk + j
        zsrc = jnp.where(foreign == 1, partner, z)
        col = pl.multiple_of(zsrc * (G * width) + a * width + c * cw, HEAD)
        src = obuf.at[u, pl.ds(j * T, T), :]
        dst = out_ref.at[:, pl.ds(col, cw)]
        idx = (zsrc * G + a) * nch + c
        remote = pltpu.make_async_remote_copy(
            src_ref=src, dst_ref=dst, send_sem=osend.at[u * per_blk + j], recv_sem=orecv.at[idx],
            device_id=(k * G + b, dest), device_id_type=MESH)
        local = pltpu.make_async_copy(src, dst, orecv.at[idx])
        mine = jnp.logical_and(b == a, dest == z)
        return mine, remote, local

    def send_out(u):
        for j in range(per_blk):
            mine, remote, local = out_copy(u, j)

            @pl.when(mine)
            def _():
                local.start()

            @pl.when(jnp.logical_not(mine))
            def _():
                remote.start()

    def open_block(u):
        blk = u // nch

        @pl.when(blk == 1)
        def _():
            wait_late()

        if swap and back >= 2:
            @pl.when(jnp.logical_and(hands_on, blk == 1))
            def _():
                for which in range(2):
                    for b in range(G):
                        moved_wait(2, b, which)
                        hand_copy(b, which).start()

        if swap:
            @pl.when(jnp.logical_and(swapped, blk == nblk // nbm))
            def _():
                wait_moved()
                for b in range(G):
                    q_wait(b, nbm - 1 - mine_half)
                    rotate_queries(b, nbm - 1 - mine_half, mine_half)

        make_bias(u)

    make_bias(0)
    scores(0, sc0, mx0)
    wait_early(1)

    def one_step(u, carry):
        @pl.when(jnp.logical_and((u + 1) % nch == 0, u + 1 < units))
        def _():
            open_block(u + 1)

        attend(u, sc0, mx0)
        scores(jnp.minimum(u + 1, units - 1), sc0, mx0)
        send_out(u)
        return carry

    lax.fori_loop(0, units, one_step, 0)

    for i in range(1, G):
        for which in (1, 0):
            kv_copy(0, i, which).wait_send()
        for p in range(nbm):
            @pl.when(chip_kept(i, p))
            def _():
                chip_q(i, p).wait_send()
    for d in range(1, back + 1):
        @pl.when(sends(d))
        def _():
            for i in range(G):
                for which in (1, 0):
                    kv_copy(d, i, which).wait_send()
    if back >= 2:
        @pl.when(relays)
        def _():
            for which in range(2):
                relay_copy(G - 1, which).wait_send()
    if swap:
        @pl.when(inner)
        def _():
            if back >= 2:
                @pl.when(hands_on)
                def _():
                    for which in range(2):
                        for b in range(G):
                            hand_copy(b, which).wait_send()

            cross_q().wait_send()
            for which in range(2):
                cross_kv(which).wait_send()
                for d in range(back + 1):
                    @pl.when(passes(d))
                    def _():
                        pass_copy(d, which).wait_send()

    def end_send(u, carry):
        for j in range(per_blk):
            mine, remote, local = out_copy(u, j)

            @pl.when(jnp.logical_not(mine))
            def _():
                remote.wait_send()
        return carry

    lax.fori_loop(0, units, end_send, 0)

    def end_recv(i, carry):
        col = pl.multiple_of(i * cw, HEAD)
        ref = out_ref.at[:, pl.ds(col, cw)]
        pltpu.make_async_copy(ref, ref, orecv.at[i]).wait()
        return carry

    lax.fori_loop(0, n_head * G * nch, end_recv, 0)


def solution(mesh):
    n_srv, n_head = mesh.shape["srv"], mesh.shape["head"]

    def body(queries, key_value_pair, lengths):
        tok, qw = queries.shape
        kv_all = key_value_pair.shape[2] // HEAD
        G = 2 if kv_all % 2 == 0 and n_srv % 2 == 0 else 1
        kvh = kv_all // G
        per = qw // HEAD // kv_all
        grp = G * tok
        n_grp = n_srv // G
        back = n_grp // 2
        T = tok // n_head
        R = max(tok // 2, T)
        chunk = per // 4
        ndoc = lengths.shape[0]
        heads = kvh * per
        nch = heads // chunk
        units = (grp // R) * nch
        W = back * grp + R
        swap = True and G == 2 and n_head % 2 == 0 and tok // R == 2
        cfg = (n_srv, n_head, G, back, tok, kvh, per, R, chunk, ndoc, swap)
        bf = jnp.bfloat16
        dma = pltpu.SemaphoreType.DMA
        return pl.pallas_call(
            functools.partial(kernel, cfg),
            out_shape=pltpu.VMEM((T, qw * n_head), bf),
            in_specs=[
                pl.BlockSpec(memory_space=pltpu.SMEM),
                pl.BlockSpec(memory_space=pl.ANY),
                pl.BlockSpec(memory_space=pl.ANY),
            ],
            out_specs=pl.BlockSpec(memory_space=pl.ANY),
            scratch_shapes=[
                pltpu.VMEM((G, tok // R, R, heads * HEAD), bf),
                pltpu.VMEM((heads, grp, HEAD), bf),
                pltpu.VMEM((2, 2, (back + 1) * grp, kvh * HEAD), bf),
                pltpu.VMEM((2, tok, kv_all * HEAD), bf),
                pltpu.VMEM((tok, kv_all * HEAD), bf),
                pltpu.VMEM((2, tok, kvh * HEAD), bf),
                pltpu.VMEM((G, 2, tok, HEAD), jnp.float32),
                pltpu.VMEM((R, W), jnp.float32),
                pltpu.VMEM((chunk * R, W), jnp.float32),
                pltpu.VMEM((chunk * R, HEAD), jnp.float32),
                pltpu.VMEM((units, R, chunk * HEAD), bf),
                dma((1,)),
                dma((G, tok // R)),
                dma((G, tok // R)),
                dma((back + 1, G, 2)),
                dma((back + 1, G, 2)),
                dma((G, 2)),
                dma((3,)),
                dma((2,)),
                dma((back + 1, 2)),
                dma((back + 1, G, 2)),
                dma((G, 2)),
                dma((units * (R // T),)),
                dma((n_head * G * nch,)),
            ],
            compiler_params=pltpu.CompilerParams(collective_id=0, has_side_effects=True),
            name="attend",
        )(lengths, queries, key_value_pair)

    in_specs = (P("srv", "head"), P(None, "srv", "head"), P())
    out_specs = P(("srv", "head"), None)
    return jax.shard_map(body, mesh=mesh, in_specs=in_specs, out_specs=out_specs, check_vma=False)
```

time: 37 us -> 34.6 us (0.935)
  the two profiles are of different devices: /device:TPU:10 before, /device:TPU:0 now
where the time goes in v1:
time: 34.6 us; the launch traced here: 34.4 us
  Pallas kernels  33.5 us (97%)
  local copies, waits for them, and re-layouts  0.97 us (3%)
    pallas_call x1, Pallas kernels, body(): pl.pallas_call(functools.partial(kernel, cfg), out_shape=pltpu.VMEM((T, q...  33.5 us
    unnamed x1, local copies, waits for them, and re-layouts  0.97 us

profile of v1, /device:TPU:0, one launch (start us, length us, event | category | flops | bytes accessed | tf_op | source)
XLA Modules:
  0.0 34.4 jit_solution(10377205974855876528)
XLA Ops:
  0.0 33.5 %attend.1 = bf16[64,8192]{1,0:T(8,128)(2,1)S(1)} custom-call(s32[8]{0:T(128)} %len_ref.1, bf16[256,2048]{1,0:T(8,128)(2,1)} %q_ref.1, bf16[2,256,256]{2,1,0:T(8,128)(2,1)} %kv_ref.1), custom_call_target="tpu_custom_call" | custom-call | tf_op jit(solution)/shard_map/attend/pallas_call | solution.py:563
  33.5 1.0 %copy.5 = bf16[64,8192]{1,0:T(8,128)(2,1)} copy(bf16[64,8192]{1,0:T(8,128)(2,1)S(1)} %attend.1) | data formatting | bytes 2097152

commit v2 on v1

--- a/solution.py
+++ b/solution.py
@@ -9,6 +9,7 @@
 from jax.sharding import PartitionSpec as P
 
 HEAD = 128
+ORDS = ((0, 2, 3, 1), (2, 0, 1, 3), (0, 2, 3, 1), (0, 2, 3, 1), (2, 3, 0, 1), (0, 2, 3, 1))
 MESH = pl.DeviceIdType.MESH
 
 
@@ -41,7 +42,8 @@
         inner = jnp.logical_or(z == n_head // 2 - 1, z == n_head // 2)
     else:
         inner = z < 0
-    swapped = jnp.logical_and(inner, a == G - 1)
+    serves = inner
+    swapped = jnp.logical_and(serves, a == G - 1)
 
     bar = pltpu.get_barrier_semaphore()
 
@@ -208,16 +210,19 @@
 
     def chip_kept(i, p):
         b = (a + i) % G
-        away = jnp.logical_and(jnp.logical_and(inner, b == G - 1), mine_half != p)
+        away = jnp.logical_and(jnp.logical_and(serves, b == G - 1), mine_half != p)
         return jnp.logical_not(away)
 
+    if swap:
+        @pl.when(inner)
+        def _():
+            cross_kv(0).start()
+            cross_kv(1).start()
     for d in range(1, back + 1):
         start_kv(d, a == G - 1 if d == back else True)
     if swap:
-        @pl.when(inner)
-        def _():
-            cross_kv(0).start()
-            cross_kv(1).start()
+        @pl.when(serves)
+        def _():
             cross_q().start()
     for i in range(1, G):
         for which in range(2):
@@ -252,12 +257,12 @@
                 kvbuf[sel, :, pl.ds((back - d) * grp, grp), :] = jnp.zeros((2, grp, kw), jnp.bfloat16)
 
     take_queries(a)
-    start_kv(back, a < G - 1)
     for i in range(1, G):
         b = (a + i) % G
         make_table(b)
         take_queries(b)
 
+    start_kv(back, a < G - 1)
     def pass_copy(d, which):
         rows = pl.ds(pl.multiple_of((back - d) * grp + a * tok, tok), tok)
         return pltpu.make_async_remote_copy(
@@ -356,12 +361,27 @@
     outer = jnp.logical_or(z < edge, z >= n_head - edge)
     scale = HEAD ** -0.5 * math.log2(math.e)
 
+    def pick(blk, order):
+        out = jnp.int32(order[-1])
+        for i in range(len(order) - 1):
+            out = jnp.where(blk == i, order[i], out)
+        return out
+
+    def order_of(blk):
+        if nblk != 4:
+            return blk
+        def both(i):
+            return jnp.where(k == 0, pick(blk, ORDS[3 + i]), pick(blk, ORDS[i]))
+
+        outer_blk = jnp.where(mine_half == 0, both(0), both(2))
+        low = jnp.logical_and(jnp.logical_and(inner, mine_half == 0), a < G - 1)
+        return jnp.where(outer, outer_blk, jnp.where(low, both(1), blk))
+
     def where_of(u):
         blk = u // nch
         c = u % nch
-        late = jnp.where(blk == 0, 0, jnp.where(blk == nblk - 1, 1, blk + 1))
-        blk = jnp.where(outer, late, blk)
-        b = G - 1 - blk % G
+        blk = order_of(blk)
+        b = jnp.where(k == 0, blk % G, G - 1 - blk % G)
         slot = (mine_half + jnp.where(swapped, 0, 1) + blk // G) % nbm
         foreign = jnp.where(jnp.logical_and(swapped, slot != mine_half), 1, 0)
         part = jnp.where(foreign == 1, mine_half, slot)
@@ -427,6 +447,13 @@
         mine = jnp.logical_and(b == a, dest == z)
         return mine, remote, local
 
+    def held(u, j):
+        if j < per_blk - 1 or nblk != 4 or per_blk < 2:
+            return u < 0
+        c, b, slot, part, foreign = where_of(u)
+        plain = jnp.logical_not(swapped)
+        return jnp.logical_and(jnp.logical_and(plain, jnp.logical_or(k == 0, u >= 2 * nch)), jnp.logical_and(mine_half == 1, part == 0))
+
     def send_out(u):
         for j in range(per_blk):
             mine, remote, local = out_copy(u, j)
@@ -435,9 +462,17 @@
             def _():
                 local.start()
 
-            @pl.when(jnp.logical_not(mine))
+            @pl.when(jnp.logical_not(jnp.logical_or(mine, held(u, j))))
             def _():
                 remote.start()
+
+    def send_held(i, carry):
+        u = i
+
+        @pl.when(held(u, per_blk - 1))
+        def _():
+            out_copy(u, per_blk - 1)[1].start()
+        return carry
 
     def open_block(u):
         blk = u // nch
@@ -446,29 +481,29 @@
         def _():
             wait_late()
 
+        if swap:
+            @pl.when(jnp.logical_and(swapped, blk == nblk // nbm))
+            def _():
+                wait_moved()
+                for b in range(G):
+                    q_wait(b, nbm - 1 - mine_half)
+                    rotate_queries(b, nbm - 1 - mine_half, mine_half)
+
+        make_bias(u)
+
+    make_bias(0)
+    scores(0, sc0, mx0)
+    wait_early(1)
+
+    def one_step(u, carry):
         if swap and back >= 2:
-            @pl.when(jnp.logical_and(hands_on, blk == 1))
+            @pl.when(jnp.logical_and(hands_on, u == nch // 2))
             def _():
                 for which in range(2):
                     for b in range(G):
                         moved_wait(2, b, which)
                         hand_copy(b, which).start()
 
-        if swap:
-            @pl.when(jnp.logical_and(swapped, blk == nblk // nbm))
-            def _():
-                wait_moved()
-                for b in range(G):
-                    q_wait(b, nbm - 1 - mine_half)
-                    rotate_queries(b, nbm - 1 - mine_half, mine_half)
-
-        make_bias(u)
-
-    make_bias(0)
-    scores(0, sc0, mx0)
-    wait_early(1)
-
-    def one_step(u, carry):
         @pl.when(jnp.logical_and((u + 1) % nch == 0, u + 1 < units))
         def _():
             open_block(u + 1)
@@ -479,6 +514,7 @@
         return carry
 
     lax.fori_loop(0, units, one_step, 0)
+    lax.fori_loop(0, units, send_held, 0)
 
     for i in range(1, G):
         for which in (1, 0):
@@ -508,7 +544,10 @@
                         for b in range(G):
                             hand_copy(b, which).wait_send()
 
-            cross_q().wait_send()
+            @pl.when(serves)
+            def _():
+                cross_q().wait_send()
+
             for which in range(2):
                 cross_kv(which).wait_send()
                 for d in range(back + 1):

time: 34.6 us -> 33 us (0.954)
  the two profiles are of different devices: /device:TPU:0 before, /device:TPU:28 now
where the time goes in v2:
time: 33 us; the launch traced here: 32.9 us
  Pallas kernels  31.9 us (97%)
  local copies, waits for them, and re-layouts  0.97 us (3%)
    pallas_call x1, Pallas kernels, body(): pl.pallas_call(functools.partial(kernel, cfg), out_shape=pltpu.VMEM((T, q...  31.9 us
    unnamed x1, local copies, waits for them, and re-layouts  0.97 us

profile of v2, /device:TPU:28, one launch (start us, length us, event | category | flops | bytes accessed | tf_op | source)
XLA Modules:
  0.0 32.9 jit_solution(12457519217006722929)
XLA Ops:
  0.0 31.9 %attend.1 = bf16[64,8192]{1,0:T(8,128)(2,1)S(1)} custom-call(s32[8]{0:T(128)} %len_ref.1, bf16[256,2048]{1,0:T(8,128)(2,1)} %q_ref.1, bf16[2,256,256]{2,1,0:T(8,128)(2,1)} %kv_ref.1), custom_call_target="tpu_custom_call" | custom-call | tf_op jit(solution)/shard_map/attend/pallas_call | solution.py:602
  31.9 1.0 %copy.5 = bf16[64,8192]{1,0:T(8,128)(2,1)} copy(bf16[64,8192]{1,0:T(8,128)(2,1)S(1)} %attend.1) | data formatting | bytes 2097152

commit v3 on v2

--- a/solution.py
+++ b/solution.py
@@ -14,7 +14,7 @@
 
 
 def kernel(cfg, len_ref, q_ref, kv_ref, out_ref, qraw, qrot, kvbuf, kvin, ksend, fkv, table, bias,
-           sc0, mx0, obuf, lsem, qs, qr, kvs, kvr, fwd, xs, xr, fs, fr, hs, osend, orecv):
+           sc0, mx0, obuf, lsem, qs, qr, kvs, kvr, fwd, xs, xr, fs, fr, hs, far, osend, orecv):
     n_srv, n_head, G, back, tok, kvh, per, R, chunk, ndoc, swap = cfg
     heads = kvh * per
     grp = G * tok
@@ -47,12 +47,46 @@
 
     bar = pltpu.get_barrier_semaphore()
 
+    own_kv = pltpu.make_async_copy(kv_ref, kvin, lsem.at[0])
+    own_kv.start()
+
+    def cols_of(b):
+        return pl.ds(pl.multiple_of(b * width, HEAD), width)
+
+    def part_rows(p):
+        return slice(p * R, (p + 1) * R)
+
+    def own_q(p):
+        return pltpu.make_async_copy(q_ref.at[part_rows(p), cols_of(a)], qraw.at[a, p], qr.at[a, p])
+
+    def kept(p):
+        return jnp.logical_not(jnp.logical_and(swapped, mine_half != p))
+
+    for p in range(nbm):
+        @pl.when(kept(p))
+        def _():
+            own_q(p).start()
+
     def greet(s, h):
         pl.semaphore_signal(bar, inc=1, device_id=(s, h), device_id_type=MESH)
 
-    for i in range(1, n_head):
-        for b in range(G):
-            greet(k * G + b, (z + i) % n_head)
+    chain = swap and n_head == 4
+    outward = jnp.where(mine_half == 0, 0, n_head - 1)
+    if chain:
+        @pl.when(inner)
+        def _():
+            for b in range(G):
+                greet(k * G + b, partner)
+                greet(k * G + b, outward)
+
+        @pl.when(jnp.logical_not(inner))
+        def _():
+            for b in range(G):
+                greet(k * G + b, jnp.where(mine_half == 0, 1, n_head - 2))
+    else:
+        for i in range(1, n_head):
+            for b in range(G):
+                greet(k * G + b, (z + i) % n_head)
     for i in range(1, G):
         greet(k * G + (a + i) % G, z)
     for d in range(1, back + 1):
@@ -65,26 +99,6 @@
         def _():
             for b in range(G):
                 greet((k - d) * G + b, z)
-
-    own_kv = pltpu.make_async_copy(kv_ref, kvin, lsem.at[0])
-    own_kv.start()
-
-    def cols_of(b):
-        return pl.ds(pl.multiple_of(b * width, HEAD), width)
-
-    def part_rows(p):
-        return slice(p * R, (p + 1) * R)
-
-    def own_q(p):
-        return pltpu.make_async_copy(q_ref.at[part_rows(p), cols_of(a)], qraw.at[a, p], qr.at[a, p])
-
-    def kept(p):
-        return jnp.logical_not(jnp.logical_and(swapped, mine_half != p))
-
-    for p in range(nbm):
-        @pl.when(kept(p))
-        def _():
-            own_q(p).start()
 
     ends = []
     total = jnp.int32(0)
@@ -140,10 +154,19 @@
     kvbuf[0, 0, own_rows, :] = ksend[:, kv_cols]
     kvbuf[0, 1, own_rows, :] = kvin[1, :, kv_cols]
 
-    count = (n_head - 1) * G + (G - 1)
+    count = (jnp.where(inner, 2, 1) if chain else n_head - 1) * G + (G - 1)
     for d in range(1, back + 1):
         count = count + G * jnp.where(k + d < n_grp, 1, 0) + G * jnp.where(k - d >= 0, 1, 0)
     pl.semaphore_wait(bar, count)
+
+    def tell(h):
+        pl.semaphore_signal(far, inc=1, device_id=(srv, h), device_id_type=MESH)
+
+    if chain:
+        @pl.when(inner)
+        def _():
+            tell(partner)
+            tell(outward)
 
     def kv_copy(d, i, which):
         b = (a + i) % G
@@ -218,12 +241,9 @@
         def _():
             cross_kv(0).start()
             cross_kv(1).start()
+            cross_q().start()
     for d in range(1, back + 1):
         start_kv(d, a == G - 1 if d == back else True)
-    if swap:
-        @pl.when(serves)
-        def _():
-            cross_q().start()
     for i in range(1, G):
         for which in range(2):
             kv_copy(0, i, which).start()
@@ -354,6 +374,16 @@
             for b in range(G - 1):
                 for which in range(2):
                     kv_wait_new(back, b, which)
+
+    if chain:
+        @pl.when(inner)
+        def _():
+            pl.semaphore_wait(far, 1)
+            tell(outward)
+
+        @pl.when(jnp.logical_not(inner))
+        def _():
+            pl.semaphore_wait(far, 2)
 
     wait_early(0)
 
@@ -452,7 +482,7 @@
             return u < 0
         c, b, slot, part, foreign = where_of(u)
         plain = jnp.logical_not(swapped)
-        return jnp.logical_and(jnp.logical_and(plain, jnp.logical_or(k == 0, u >= 2 * nch)), jnp.logical_and(mine_half == 1, part == 0))
+        return jnp.logical_and(jnp.logical_and(plain, u >= jnp.where(k == 0, nch, 2 * nch)), jnp.logical_and(mine_half == 1, part == 0))
 
     def send_out(u):
         for j in range(per_blk):
@@ -631,6 +661,7 @@
                 dma((back + 1, 2)),
                 dma((back + 1, G, 2)),
                 dma((G, 2)),
+                pltpu.SemaphoreType.REGULAR,
                 dma((units * (R // T),)),
                 dma((n_head * G * nch,)),
             ],

time: 33 us -> 32.9 us (level)
  the two profiles are of different devices: /device:TPU:28 before, /device:TPU:10 now
where the time goes in v3:
time: 32.9 us; the launch traced here: 32.3 us
  Pallas kernels  31.3 us (95%)
  local copies, waits for them, and re-layouts  0.97 us (3%)
    pallas_call x1, Pallas kernels, body(): pl.pallas_call(functools.partial(kernel, cfg), out_shape=pltpu.VMEM((T, q...  31.3 us
    unnamed x1, local copies, waits for them, and re-layouts  0.97 us

profile of v3, /device:TPU:10, one launch (start us, length us, event | category | flops | bytes accessed | tf_op | source)
XLA Modules:
  0.0 32.3 jit_solution(9177883687595877509)
XLA Ops:
  0.0 31.3 %attend.1 = bf16[64,8192]{1,0:T(8,128)(2,1)S(1)} custom-call(s32[8]{0:T(128)} %len_ref.1, bf16[256,2048]{1,0:T(8,128)(2,1)} %q_ref.1, bf16[2,256,256]{2,1,0:T(8,128)(2,1)} %kv_ref.1), custom_call_target="tpu_custom_call" | custom-call | tf_op jit(solution)/shard_map/attend/pallas_call | solution.py:632
  31.4 1.0 %copy.5 = bf16[64,8192]{1,0:T(8,128)(2,1)} copy(bf16[64,8192]{1,0:T(8,128)(2,1)S(1)} %attend.1) | data formatting | bytes 2097152

commit v4 on v3

--- a/solution.py
+++ b/solution.py
@@ -72,17 +72,16 @@
 
     chain = swap and n_head == 4
     outward = jnp.where(mine_half == 0, 0, n_head - 1)
+    first_inner = z == n_head // 2 - 1
     if chain:
-        @pl.when(inner)
-        def _():
-            for b in range(G):
-                greet(k * G + b, partner)
-                greet(k * G + b, outward)
-
-        @pl.when(jnp.logical_not(inner))
-        def _():
-            for b in range(G):
-                greet(k * G + b, jnp.where(mine_half == 0, 1, n_head - 2))
+        for b in range(G):
+            @pl.when(z < n_head - 1)
+            def _():
+                greet(k * G + b, z + 1)
+
+            @pl.when(z == n_head // 2)
+            def _():
+                greet(k * G + b, z - 1)
     else:
         for i in range(1, n_head):
             for b in range(G):
@@ -154,7 +153,10 @@
     kvbuf[0, 0, own_rows, :] = ksend[:, kv_cols]
     kvbuf[0, 1, own_rows, :] = kvin[1, :, kv_cols]
 
-    count = (jnp.where(inner, 2, 1) if chain else n_head - 1) * G + (G - 1)
+    if chain:
+        count = jnp.where(first_inner, 2, jnp.where(z == 0, 0, 1)) * G + (G - 1)
+    else:
+        count = (n_head - 1) * G + (G - 1)
     for d in range(1, back + 1):
         count = count + G * jnp.where(k + d < n_grp, 1, 0) + G * jnp.where(k - d >= 0, 1, 0)
     pl.semaphore_wait(bar, count)
@@ -162,11 +164,15 @@
     def tell(h):
         pl.semaphore_signal(far, inc=1, device_id=(srv, h), device_id_type=MESH)
 
-    if chain:
-        @pl.when(inner)
-        def _():
-            tell(partner)
-            tell(outward)
+    def say_in():
+        @pl.when(first_inner)
+        def _():
+            tell(0)
+            tell(z + 1)
+
+        @pl.when(z == n_head - 1)
+        def _():
+            tell(z - 1)
 
     def kv_copy(d, i, which):
         b = (a + i) % G
@@ -242,6 +248,8 @@
             cross_kv(0).start()
             cross_kv(1).start()
             cross_q().start()
+    if chain:
+        say_in()
     for d in range(1, back + 1):
         start_kv(d, a == G - 1 if d == back else True)
     for i in range(1, G):
@@ -376,14 +384,24 @@
                     kv_wait_new(back, b, which)
 
     if chain:
-        @pl.when(inner)
+        @pl.when(z == n_head // 2)
+        def _():
+            pl.semaphore_wait(far, 2)
+            tell(z - 1)
+            tell(z + 1)
+
+        @pl.when(first_inner)
         def _():
             pl.semaphore_wait(far, 1)
-            tell(outward)
-
-        @pl.when(jnp.logical_not(inner))
+            tell(0)
+
+        @pl.when(z == 0)
         def _():
             pl.semaphore_wait(far, 2)
+
+        @pl.when(z == n_head - 1)
+        def _():
+            pl.semaphore_wait(far, 1)
 
     wait_early(0)
 
@@ -469,11 +487,10 @@
         col = pl.multiple_of(zsrc * (G * width) + a * width + c * cw, HEAD)
         src = obuf.at[u, pl.ds(j * T, T), :]
         dst = out_ref.at[:, pl.ds(col, cw)]
-        idx = (zsrc * G + a) * nch + c
         remote = pltpu.make_async_remote_copy(
-            src_ref=src, dst_ref=dst, send_sem=osend.at[u * per_blk + j], recv_sem=orecv.at[idx],
+            src_ref=src, dst_ref=dst, send_sem=osend.at[u * per_blk + j], recv_sem=orecv.at[0],
             device_id=(k * G + b, dest), device_id_type=MESH)
-        local = pltpu.make_async_copy(src, dst, orecv.at[idx])
+        local = pltpu.make_async_copy(src, dst, orecv.at[0])
         mine = jnp.logical_and(b == a, dest == z)
         return mine, remote, local
 
@@ -482,7 +499,7 @@
             return u < 0
         c, b, slot, part, foreign = where_of(u)
         plain = jnp.logical_not(swapped)
-        return jnp.logical_and(jnp.logical_and(plain, u >= jnp.where(k == 0, nch, 2 * nch)), jnp.logical_and(mine_half == 1, part == 0))
+        return jnp.logical_and(jnp.logical_and(plain, u >= jnp.where(k == 0, nch // 2, 2 * nch)), jnp.logical_and(mine_half == 1, part == 0))
 
     def send_out(u):
         for j in range(per_blk):
@@ -596,13 +613,7 @@
 
     lax.fori_loop(0, units, end_send, 0)
 
-    def end_recv(i, carry):
-        col = pl.multiple_of(i * cw, HEAD)
-        ref = out_ref.at[:, pl.ds(col, cw)]
-        pltpu.make_async_copy(ref, ref, orecv.at[i]).wait()
-        return carry
-
-    lax.fori_loop(0, n_head * G * nch, end_recv, 0)
+    pltpu.make_async_copy(out_ref, out_ref, orecv.at[0]).wait()
 
 
 def solution(mesh):
@@ -663,7 +674,7 @@
                 dma((G, 2)),
                 pltpu.SemaphoreType.REGULAR,
                 dma((units * (R // T),)),
-                dma((n_head * G * nch,)),
+                dma((1,)),
             ],
             compiler_params=pltpu.CompilerParams(collective_id=0, has_side_effects=True),
             name="attend",

time: 32.9 us -> 32.2 us (0.979); the launches traced: 32.3 us -> 32 us
  no operation moved by 1% of the time
where the time goes in v4:
time: 32.2 us; the launch traced here: 32 us
  Pallas kernels  31.1 us (97%)
  local copies, waits for them, and re-layouts  0.97 us (3%)
    pallas_call x1, Pallas kernels, body(): pl.pallas_call(functools.partial(kernel, cfg), out_shape=pltpu.VMEM((T, q...  31.1 us
    unnamed x1, local copies, waits for them, and re-layouts  0.97 us

profile of v4, /device:TPU:10, one launch (start us, length us, event | category | flops | bytes accessed | tf_op | source)
XLA Modules:
  0.0 32.0 jit_solution(14042726176008052023)
XLA Ops:
  0.0 31.1 %attend.1 = bf16[64,8192]{1,0:T(8,128)(2,1)S(1)} custom-call(s32[8]{0:T(128)} %len_ref.1, bf16[256,2048]{1,0:T(8,128)(2,1)} %q_ref.1, bf16[2,256,256]{2,1,0:T(8,128)(2,1)} %kv_ref.1), custom_call_target="tpu_custom_call" | custom-call | tf_op jit(solution)/shard_map/attend/pallas_call | solution.py:643
  31.1 1.0 %copy.5 = bf16[64,8192]{1,0:T(8,128)(2,1)} copy(bf16[64,8192]{1,0:T(8,128)(2,1)S(1)} %attend.1) | data formatting | bytes 2097152

commit v5 on v4

--- a/solution.py
+++ b/solution.py
@@ -47,8 +47,9 @@
 
     bar = pltpu.get_barrier_semaphore()
 
-    own_kv = pltpu.make_async_copy(kv_ref, kvin, lsem.at[0])
-    own_kv.start()
+    own_kv = [pltpu.make_async_copy(kv_ref.at[i], kvin.at[i], lsem.at[i]) for i in range(2)]
+    for c in own_kv:
+        c.start()
 
     def cols_of(b):
         return pl.ds(pl.multiple_of(b * width, HEAD), width)
@@ -143,15 +144,14 @@
         return (x * cosine + pltpu.roll(x, HEAD // 2, 1) * sine).astype(jnp.bfloat16)
 
     make_table(a)
-    own_kv.wait()
+    own_kv[0].wait()
     for h in range(G * kvh):
         cols = slice(h * HEAD, (h + 1) * HEAD)
         ksend[:, cols] = rotate(kvin[0, :, cols], table[a, 0], table[a, 1])
 
     own_rows = pl.ds(pl.multiple_of(back * grp + a * tok, tok), tok)
     kv_cols = pl.ds(pl.multiple_of(a * kw, HEAD), kw)
-    kvbuf[0, 0, own_rows, :] = ksend[:, kv_cols]
-    kvbuf[0, 1, own_rows, :] = kvin[1, :, kv_cols]
+    own_kv[1].wait()
 
     if chain:
         count = jnp.where(first_inner, 2, jnp.where(z == 0, 0, 1)) * G + (G - 1)
@@ -284,6 +284,8 @@
             for sel in range(2 if swap else 1):
                 kvbuf[sel, :, pl.ds((back - d) * grp, grp), :] = jnp.zeros((2, grp, kw), jnp.bfloat16)
 
+    kvbuf[0, 0, own_rows, :] = ksend[:, kv_cols]
+    kvbuf[0, 1, own_rows, :] = kvin[1, :, kv_cols]
     take_queries(a)
     for i in range(1, G):
         b = (a + i) % G
@@ -661,7 +663,7 @@
                 pltpu.VMEM((chunk * R, W), jnp.float32),
                 pltpu.VMEM((chunk * R, HEAD), jnp.float32),
                 pltpu.VMEM((units, R, chunk * HEAD), bf),
-                dma((1,)),
+                dma((2,)),
                 dma((G, tok // R)),
                 dma((G, tok // R)),
                 dma((back + 1, G, 2)),

time: 32.2 us -> 32.2 us (level)
  no operation moved by 1% of the time
where the time goes in v5:
time: 32.2 us; the launch traced here: 32.1 us
  Pallas kernels  31.1 us (97%)
  local copies, waits for them, and re-layouts  0.97 us (3%)
    pallas_call x1, Pallas kernels, body(): pl.pallas_call(functools.partial(kernel, cfg), out_shape=pltpu.VMEM((T, q...  31.1 us
    unnamed x1, local copies, waits for them, and re-layouts  0.97 us

profile of v5, /device:TPU:10, one launch (start us, length us, event | category | flops | bytes accessed | tf_op | source)
XLA Modules:
  0.0 32.1 jit_solution(8818643002548708112)
XLA Ops:
  0.0 31.1 %attend.1 = bf16[64,8192]{1,0:T(8,128)(2,1)S(1)} custom-call(s32[8]{0:T(128)} %len_ref.1, bf16[256,2048]{1,0:T(8,128)(2,1)} %q_ref.1, bf16[2,256,256]{2,1,0:T(8,128)(2,1)} %kv_ref.1), custom_call_target="tpu_custom_call" | custom-call | tf_op jit(solution)/shard_map/attend/pallas_call | solution.py:645
  31.1 1.0 %copy.5 = bf16[64,8192]{1,0:T(8,128)(2,1)} copy(bf16[64,8192]{1,0:T(8,128)(2,1)S(1)} %attend.1) | data formatting | bytes 2097152

commit v6 on v5

--- a/solution.py
+++ b/solution.py
@@ -562,7 +562,10 @@
         send_out(u)
         return carry
 
-    lax.fori_loop(0, units, one_step, 0)
+    attend(0, sc0, mx0)
+    send_out(0)
+    scores(1, sc0, mx0)
+    lax.fori_loop(1, units, one_step, 0)
     lax.fori_loop(0, units, send_held, 0)
 
     for i in range(1, G):

time: 32.2 us -> 32.2 us (level)
  no operation moved by 1% of the time
where the time goes in v6:
time: 32.2 us; the launch traced here: 32 us
  Pallas kernels  31 us (96%)
  local copies, waits for them, and re-layouts  0.97 us (3%)
    pallas_call x1, Pallas kernels, body(): pl.pallas_call(functools.partial(kernel, cfg), out_shape=pltpu.VMEM((T, q...  31 us
    unnamed x1, local copies, waits for them, and re-layouts  0.97 us

profile of v6, /device:TPU:10, one launch (start us, length us, event | category | flops | bytes accessed | tf_op | source)
XLA Modules:
  0.0 32.0 jit_solution(1520514301400404862)
XLA Ops:
  0.0 31.0 %attend.1 = bf16[64,8192]{1,0:T(8,128)(2,1)S(1)} custom-call(s32[8]{0:T(128)} %len_ref.1, bf16[256,2048]{1,0:T(8,128)(2,1)} %q_ref.1, bf16[2,256,256]{2,1,0:T(8,128)(2,1)} %kv_ref.1), custom_call_target="tpu_custom_call" | custom-call | tf_op jit(solution)/shard_map/attend/pallas_call | solution.py:648
  31.0 1.0 %copy.5 = bf16[64,8192]{1,0:T(8,128)(2,1)} copy(bf16[64,8192]{1,0:T(8,128)(2,1)S(1)} %attend.1) | data formatting | bytes 2097152
